TPU v7x, 32 devices: a whole 2x2x4 slice. The times are simulated.
32 devices in a mesh: space: 8 (over z, x), chan: 4 (over y, core).
Axes of the slice: x: 2, y: 2, z: 4, core: 2. Of those that a mesh axis runs over, the one named last changes fastest.
Arguments:
- features: bfloat16 [256, 8, 1024], P('chan', 'space'), may hold values from -6 to 6
- filters: bfloat16 [27, 256, 256], P(None, 'chan'), may hold values from -0.078125 to 0.078125
- out_bias: float32 [256], P('chan'), may hold values from -1 to 1
- loss_grad: bfloat16 [256, 8, 1024], P('chan', 'space'), may hold values from -6 to 6
Outputs:
- activated: float32 [256, 8, 1024], P('chan', 'space')
- in_grad: float32 [256, 8, 1024], P('chan', 'space')
- filter_grad: float32 [27, 256, 256], P(None, 'chan')
- bias_grad: float32 [256], replicated
All inputs are finite; a program needn't handle non-finite values.
Results may differ from a plain program's by a relative error of at most 0.0031.
Values may be sent and summed in bfloat16 or wider, within the bound.
No kernel may reach another device: no remote copies, remote signals or barrier semaphores. Data moves between devices by JAX's collectives and lax.ppermute only.
A program may use at most 128 MiB of HBM per device.

v0:
```python
import math
import jax
import jax.numpy as jnp
from jax import lax
from jax.sharding import PartitionSpec as P

TAPS = 27
PLANE_H = 32
PLANE_W = 32


def extended(cells, sides, width):
    for axis, dim in sides:
        count = lax.axis_size(axis)
        ends = count - 1
        head = lax.slice_in_dim(cells, 0, width, axis=dim)
        tail = lax.slice_in_dim(cells, cells.shape[dim] - width, cells.shape[dim], axis=dim)
        cells = jnp.concatenate(
            [
                lax.ppermute(tail, axis, [(i, (i + 1) % count) for i in range(ends)]),
                cells,
                lax.ppermute(head, axis, [((i + 1) % count, i) for i in range(ends)]),
            ],
            axis=dim,
        )
    return cells


def plane_pad(volume):
    chans, planes, cells = volume.shape
    grid = volume.reshape(chans, planes, PLANE_H, PLANE_W)
    return jnp.pad(grid, ((0, 0), (0, 0), (1, 1), (1, 1)))


def window(padded, depth_off, row_off, col_off, planes):
    chans = padded.shape[0]
    piece = lax.slice(
        padded,
        (0, depth_off, row_off, col_off),
        (chans, depth_off + planes, row_off + PLANE_H, col_off + PLANE_W),
    )
    return piece.reshape(chans, planes * PLANE_H * PLANE_W)


def contract_lead(left, right):
    return lax.dot_general(
        left, right, (((0,), (0,)), ((), ())), preferred_element_type=jnp.float32
    )


def contract_last(left, right):
    return lax.dot_general(
        left, right, (((1,), (1,)), ((), ())), preferred_element_type=jnp.float32
    )


def depth_rim(volume):
    return extended(volume, (("space", 1),), 1)


def all_channels(volume):
    return lax.all_gather(volume, "chan", axis=0, tiled=True)


def full_view(volume):
    return depth_rim(all_channels(volume))


def body(features, filters, out_bias, loss_grad):
    local_in, planes, cells = features.shape
    local_out = out_bias.shape[0]
    total_out = filters.shape[2]
    voxels = planes * cells
    offsets = [(tap // 9, tap // 3 % 3, tap % 3) for tap in range(TAPS)]
    padded_all = plane_pad(full_view(features))
    columns = lax.all_to_all(filters, "chan", split_axis=2, concat_axis=1, tiled=True)
    summed = jnp.zeros((local_out, voxels), jnp.float32)
    for tap_index, (depth_off, row_off, col_off) in enumerate(offsets):
        piece = window(padded_all, depth_off, row_off, col_off, planes)
        summed = summed + contract_lead(columns[tap_index], piece)
    padded_own = lax.dynamic_slice_in_dim(
        padded_all, lax.axis_index("chan") * local_in, local_in, 0
    )
    pre_act = summed + out_bias[:, None]
    sigmoid = jax.nn.sigmoid(pre_act)
    activated = (pre_act * sigmoid).reshape(local_out, planes, cells)
    grad_pre = (
        loss_grad.reshape(local_out, voxels).astype(jnp.float32)
        * sigmoid
        * (1.0 + pre_act * (1.0 - sigmoid))
    ).astype(jnp.bfloat16)
    grad_full = full_view(grad_pre.reshape(local_out, planes, cells))
    padded_grad = plane_pad(grad_full)
    grad_inner = lax.slice_in_dim(grad_full, 1, 1 + planes, axis=1).reshape(total_out, voxels)
    in_total = jnp.zeros((local_in, voxels), jnp.float32)
    filter_list = []
    for tap_index, (depth_off, row_off, col_off) in enumerate(offsets):
        shifted = window(padded_grad, 2 - depth_off, 2 - row_off, 2 - col_off, planes)
        in_total = in_total + jnp.dot(
            filters[tap_index], shifted, preferred_element_type=jnp.float32
        )
        piece = window(padded_own, depth_off, row_off, col_off, planes)
        filter_list.append(contract_last(piece, grad_inner))
    factor = 1.0 / math.sqrt(voxels * lax.axis_size("space"))
    filter_part = jnp.stack(filter_list, axis=0) * factor
    bias_part = jnp.sum(grad_inner.astype(jnp.float32), axis=1) * factor
    filter_grad, bias_grad = lax.psum((filter_part, bias_part), "space")
    in_grad = in_total.reshape(local_in, planes, cells)
    return (activated, in_grad, filter_grad, bias_grad)


def solution(mesh):
    in_specs = (
        P("chan", "space", None),
        P(None, "chan", None),
        P("chan"),
        P("chan", "space", None),
    )
    out_specs = (P("chan", "space", None), P("chan", "space", None), P(None, "chan", None), P())
    return jax.shard_map(body, mesh=mesh, in_specs=in_specs, out_specs=out_specs, check_vma=False)
```

profile of v0, /device:TPU:0, one launch (start us, length us, event | category | flops | bytes accessed | tf_op | source)
XLA Modules:
  0.0 211.8 jit_solution(13178048618152019697)
XLA Ops:
  7.2 9.0 %all_gather.6 = bf16[256,1,1024]{2,0,1:T(8,128)(2,1)S(1)} all-gather(bf16[64,1,1024]{2,0,1:T(8,128)(2,1)} %param.4), channel_id=1, replica_groups=mesh['space'=8,'chan'=4] {'chan'}, dimensions={0}, use_global_device_ids=true | all-gather | bytes 655360 | tf_op jit(solution)/shard_map/all_gather | solution.py:62
  16.4 1.3 collective-permute-start.1
  17.7 5.3 %collective-permute-start = (bf16[256,1,1024]{0,2,1:T(8,128)(2,1)S(1)}, bf16[256,1,1024]{0,2,1:T(8,128)(2,1)}, u32[]{:S(2)}, u32[]{:S(2)}) collective-permute-start(bf16[256,1,1024]{0,2,1:T(8,128)(2,1)S(1)} %copy.15), channel_id=1, source_target_pairs={{0,4},{4,8},{8,12},{12,16},{16,20},{20,24},{24,28},{1,5},{5,9},{9,... | collective-permute-start | bytes 1572872 | tf_op jit(solution)/shard_map/ppermute | solution.py:20
  23.0 3.0 %copy.18 = bf16[27,64,256]{1,0,2:T(8,128)(2,1)S(1)} copy(bf16[27,64,256]{2,1,0:T(8,128)(2,1)S(1)} %copy-done) | data formatting | bytes 1769472 | tf_op args[1]
  26.1 2.4 %reshape.417 = bf16[4,2,55296]{2,1,0:T(2,128)(2,1)} reshape(bf16[256,27,64]{2,1,0:T(8,128)(2,1)S(1)} %bitcast.575) | data formatting | bytes 1769472
  28.5 3.5 %all-to-all-start = ((bf16[4,2,55296]{2,1,0:T(2,128)(2,1)}), bf16[4,2,55296]{2,1,0:T(2,128)(2,1)S(1)}, u32[]{:S(2)}, u32[]{:S(2)}) async-start(bf16[4,2,55296]{2,1,0:T(2,128)(2,1)} %reshape.417), calls=%async_computation | async-start | bytes 1769472 | tf_op jit(solution)/shard_map/all_to_all | solution.py:76
  32.0 0.5 collective-permute-done.1
  32.6 11.0 %collective-permute-done = bf16[256,1,1024]{0,2,1:T(8,128)(2,1)} collective-permute-done((bf16[256,1,1024]{0,2,1:T(8,128)(2,1)S(1)}, bf16[256,1,1024]{0,2,1:T(8,128)(2,1)}, u32[]{:S(2)}, u32[]{:S(2)}) %collective-permute-start) | collective-permute-done | bytes 524320 | tf_op jit(solution)/shard_map/ppermute | solution.py:20
  43.6 1.4 pad_maximum_fusion
  45.0 3.4 %pad_dynamic-slice_fusion.15 = (bf16[64,1,32,32]{0,3,2,1:T(8,128)(2,1)}, bf16[64,1,32,32]{0,3,2,1:T(8,128)(2,1)}, bf16[64,1,32,32]{0,3,2,1:T(8,128)(2,1)}, bf16[...) fusion(s32[]{:T(128)S(6)} %select_n.3, ...), kind=kLoop, calls=%fused_computation.15 | loop fusion | bytes 3014668 | tf_op jit(solution)/shard_map/slice | solution.py:37
  48.3 4.7 %pad_dynamic-slice_fusion.26 = (bf16[64,1,32,32]{0,3,2,1:T(8,128)(2,1)}, bf16[64,1,32,32]{0,3,2,1:T(8,128)(2,1)}, bf16[64,1,32,32]{0,3,2,1:T(8,128)(2,1)}, bf16[...) fusion(s32[]{:T(128)S(6)} %select_n.3, ...), kind=kLoop, calls=%fused_computation.26 | loop fusion | bytes 3670028 | tf_op jit(solution)/shard_map/slice | solution.py:37
  53.0 2.1 pad_slice_fusion.1
  55.1 4.8 %pad_slice_fusion = (bf16[256,1,32,32]{0,3,2,1:T(8,128)(2,1)}, bf16[256,1,32,32]{0,3,2,1:T(8,128)(2,1)}, bf16[256,1,32,32]{0,3,2,1:T(8,128)(2,1)}, bf16[256,1,32...) fusion(bf16[256,3,32,32]{0,3,2,1:T(8,128)(2,1)S(1)} %bitcast.571), kind=kLoop, calls=%fused_computation.27 | loop fusion | bytes 11534336 | tf_op jit(solution)/shard_map/slice | solution.py:37
  59.9 1.9 reshape.418
  61.8 1.4 copy.24
  63.4 0.6 fusion.108
  64.0 0.7 squeeze.163
  64.8 0.7 squeeze.162
  65.5 0.7 squeeze.164
  66.2 0.7 squeeze.165
  66.9 0.7 squeeze.166
  70.2 1.0 fusion.110
  71.2 1.1 convolution_add_fusion.31
  80.8 0.3 fusion.52
  81.2 7.1 %all-gather = bf16[256,1024]{1,0:T(8,128)(2,1)S(1)} all-gather(bf16[64,1024]{1,0:T(8,128)(2,1)S(1)} %get-tuple-element.124), channel_id=2, replica_groups=mesh['space'=8,'chan'=4] {'chan'}, dimensions={0}, use_global_device_ids=true | all-gather | bytes 655360 | tf_op jit(solution)/shard_map/all_gather | solution.py:62
  88.3 1.3 collective-permute-start.3
  89.6 5.4 %collective-permute-start.2 = (bf16[256,1,1024]{2,0,1:T(8,128)(2,1)S(1)}, bf16[256,1,1024]{2,0,1:T(8,128)(2,1)S(1)}, u32[]{:S(2)}, u32[]{:S(2)}) collective-permute-start(bf16[256,1,1024]{2,0,1:T(8,128)(2,1)S(1)} %bitcast.566), channel_id=1, source_target_pairs={{0,4},{4,8},{8,12},{12,16},{16,20},{20,24},{24,28},{1,5},{5,9},{9,... | collective-permute-start | bytes 1572872 | tf_op jit(solution)/shard_map/ppermute | solution.py:20
  95.0 1.0 copy.21
  96.2 0.3 fusion.49
  97.2 0.3 fusion.46
  98.5 0.3 fusion.42
  98.8 0.3 fusion.41
  99.4 0.3 fusion.39
  99.7 0.3 fusion.38
  100.7 0.3 fusion.35
  101.0 0.3 fusion.34
  102.0 0.3 fusion.31
  102.9 0.3 fusion.28
  103.5 0.3 fusion.26
  104.2 0.3 fusion.24
  104.4 1.4 broadcast_multiply_fusion
  106.0 28.3 %psum.15 = f32[256]{0:T(256)} all-reduce(f32[256]{0:T(256)S(1)} %broadcast_multiply_fusion.1), channel_id=1, replica_groups=mesh['space'=8,'chan'=4] {'space'}, use_global_device_ids=true, to_apply=%region_2.3 | all-reduce | flops 256 | bytes 2048 | tf_op jit(solution)/shard_map/psum | solution.py:107
  134.5 0.7 copy.20
  135.2 0.9 pad_slice_fusion.25
  136.1 3.7 %pad_slice_fusion.24 = (bf16[256,1,32,32]{0,3,2,1:T(8,128)(2,1)S(1)}, bf16[256,1,32,32]{0,3,2,1:T(8,128)(2,1)S(1)}, bf16[256,1,32,32]{0,3,2,1:T(8,128)(2,1)S(1)}...) fusion(bf16[256,3,32,32]{0,3,2,1:T(8,128)(2,1)S(1)} %bitcast.573), kind=kLoop, calls=%fused_computation.51 | loop fusion | bytes 11534336 | tf_op jit(solution)/shard_map/slice | solution.py:37
  147.5 1.0 copy.22
  148.5 53.6 %all-reduce.4.cloned.1.call-done = f32[27,64,256]{2,1,0:T(8,128)} async-done(((f32[27,64,256]{2,1,0:T(8,128)}), f32[27,64,256]{2,1,0:T(8,128)}) %all-reduce.4.cloned.1.call-update) | async-done | bytes 1769488 | tf_op jit(solution)/shard_map/psum | solution.py:107
  202.1 2.9 %copy.52 = f32[27,64,256]{2,1,0:T(8,128)} copy(f32[27,64,256]{2,1,0:T(8,128)} %all-reduce.4.cloned.1.call-done) | data formatting | bytes 3538944
  (218 shorter events, 23.8 us)
Async XLA Ops:
  7.2 15.9 %copy-start = (bf16[27,64,256]{2,1,0:T(8,128)(2,1)S(1)}, bf16[27,64,256]{2,1,0:T(8,128)(2,1)}, u32[]{:S(2)}) copy-start(bf16[27,64,256]{2,1,0:T(8,128)(2,1)} %param.5) | copy-start | bytes 2654212
  16.4 16.2 %collective-permute-start.1 = (bf16[256,1,1024]{0,2,1:T(8,128)(2,1)S(1)}, bf16[256,1,1024]{0,2,1:T(8,128)(2,1)}, u32[]{:S(2)}, u32[]{:S(2)}) collective-permute-start(bf16[256,1,1024]{0,2,1:T(8,128)(2,1)S(1)} %copy.15), channel_id=1, source_target_pairs={{4,0},{8,4},{12,8},{16,12},{20,16},{24,20},{28,24},{5,1},{9,5},{13... | collective-permute-start | bytes 1572872 | tf_op jit(solution)/shard_map/ppermute | solution.py:22
  17.7 25.9 %collective-permute-start = (bf16[256,1,1024]{0,2,1:T(8,128)(2,1)S(1)}, bf16[256,1,1024]{0,2,1:T(8,128)(2,1)}, u32[]{:S(2)}, u32[]{:S(2)}) collective-permute-start(bf16[256,1,1024]{0,2,1:T(8,128)(2,1)S(1)} %copy.15), channel_id=1, source_target_pairs={{0,4},{4,8},{8,12},{12,16},{16,20},{20,24},{24,28},{1,5},{5,9},{9,... | collective-permute-start | bytes 1572872 | tf_op jit(solution)/shard_map/ppermute | solution.py:20
  28.5 31.5 %all-to-all-start = ((bf16[4,2,55296]{2,1,0:T(2,128)(2,1)}), bf16[4,2,55296]{2,1,0:T(2,128)(2,1)S(1)}, u32[]{:S(2)}, u32[]{:S(2)}) async-start(bf16[4,2,55296]{2,1,0:T(2,128)(2,1)} %reshape.417), calls=%async_computation | async-start | bytes 1769472 | tf_op jit(solution)/shard_map/all_to_all | solution.py:76
  32.0 170.1 %all-reduce.4.cloned.1.call-start = ((), (), s32[]{:S(2)}) async-start(), calls=%async_computation.1 | async-start | bytes 3538944 | tf_op jit(solution)/shard_map/psum | solution.py:107
  64.0 6.1 %copy-start.26 = (bf16[256,1,32,32]{0,3,2,1:T(8,128)(2,1)S(1)}, bf16[256,1,32,32]{0,3,2,1:T(8,128)(2,1)}, u32[]{:S(2)}) copy-start(bf16[256,1,32,32]{0,3,2,1:T(8,128)(2,1)} %get-tuple-element.98) | copy-start | bytes 1572868
  64.0 7.2 %copy-start.8 = (bf16[256,1,32,32]{0,3,2,1:T(8,128)(2,1)S(1)}, bf16[256,1,32,32]{0,3,2,1:T(8,128)(2,1)}, u32[]{:S(2)}) copy-start(bf16[256,1,32,32]{0,3,2,1:T(8,128)(2,1)} %get-tuple-element.123) | copy-start | bytes 1572868
  68.3 4.0 %copy-start.25 = (bf16[256,1,32,32]{0,3,2,1:T(8,128)(2,1)S(1)}, bf16[256,1,32,32]{0,3,2,1:T(8,128)(2,1)}, u32[]{:S(2)}) copy-start(bf16[256,1,32,32]{0,3,2,1:T(8,128)(2,1)} %get-tuple-element.99) | copy-start | bytes 1572868
  69.6 3.1 %copy-start.24 = (bf16[256,1,32,32]{0,3,2,1:T(8,128)(2,1)S(1)}, bf16[256,1,32,32]{0,3,2,1:T(8,128)(2,1)}, u32[]{:S(2)}) copy-start(bf16[256,1,32,32]{0,3,2,1:T(8,128)(2,1)} %get-tuple-element.100) | copy-start | bytes 1572868
  69.7 3.0 %copy-start.56 = (bf16[256,64]{0,1:T(8,128)(2,1)S(1)}, bf16[256,64]{0,1:T(8,128)(2,1)}, u32[]{:S(2)}) copy-start(bf16[256,64]{0,1:T(8,128)(2,1)} %squeeze.165) | copy-start | bytes 98308
  69.8 2.5 %copy-start.57 = (bf16[256,64]{0,1:T(8,128)(2,1)S(1)}, bf16[256,64]{0,1:T(8,128)(2,1)}, u32[]{:S(2)}) copy-start(bf16[256,64]{0,1:T(8,128)(2,1)} %squeeze.164) | copy-start | bytes 98308
  71.2 1.8 copy-start.7
  71.2 1.8 copy-start.55
  73.3 1.2 copy-start.20
  74.7 1.1 copy-start.16
  76.1 1.1 copy-start.13
  77.6 1.1 copy-start.9
  79.0 1.1 copy-start.2
  80.7 15.2 %copy-start.53 = (bf16[64,1,32,32]{0,3,2,1:T(8,128)(2,1)S(1)}, bf16[64,1,32,32]{0,3,2,1:T(8,128)(2,1)}, u32[]{:S(2)}) copy-start(bf16[64,1,32,32]{0,3,2,1:T(8,128)(2,1)} %get-tuple-element.69) | copy-start | bytes 393220
  80.8 15.4 %copy-start.52 = (bf16[64,1,32,32]{0,3,2,1:T(8,128)(2,1)S(1)}, bf16[64,1,32,32]{0,3,2,1:T(8,128)(2,1)}, u32[]{:S(2)}) copy-start(bf16[64,1,32,32]{0,3,2,1:T(8,128)(2,1)} %get-tuple-element.68) | copy-start | bytes 393220
  81.2 15.4 %copy-start.51 = (bf16[64,1,32,32]{0,3,2,1:T(8,128)(2,1)S(1)}, bf16[64,1,32,32]{0,3,2,1:T(8,128)(2,1)}, u32[]{:S(2)}) copy-start(bf16[64,1,32,32]{0,3,2,1:T(8,128)(2,1)} %get-tuple-element.67) | copy-start | bytes 393220
  81.2 15.7 %copy-start.50 = (bf16[64,1,32,32]{0,3,2,1:T(8,128)(2,1)S(1)}, bf16[64,1,32,32]{0,3,2,1:T(8,128)(2,1)}, u32[]{:S(2)}) copy-start(bf16[64,1,32,32]{0,3,2,1:T(8,128)(2,1)} %get-tuple-element.66) | copy-start | bytes 393220
  88.3 46.0 %collective-permute-start.3 = (bf16[256,1,1024]{2,0,1:T(8,128)(2,1)S(1)}, bf16[256,1,1024]{2,0,1:T(8,128)(2,1)S(1)}, u32[]{:S(2)}, u32[]{:S(2)}) collective-permute-start(bf16[256,1,1024]{2,0,1:T(8,128)(2,1)S(1)} %bitcast.565), channel_id=1, source_target_pairs={{4,0},{8,4},{12,8},{16,12},{20,16},{24,20},{28,24},{5,1},{9,5},{13... | collective-permute-start | bytes 1572872 | tf_op jit(solution)/shard_map/ppermute | solution.py:22
  89.6 44.7 %collective-permute-start.2 = (bf16[256,1,1024]{2,0,1:T(8,128)(2,1)S(1)}, bf16[256,1,1024]{2,0,1:T(8,128)(2,1)S(1)}, u32[]{:S(2)}, u32[]{:S(2)}) collective-permute-start(bf16[256,1,1024]{2,0,1:T(8,128)(2,1)S(1)} %bitcast.566), channel_id=1, source_target_pairs={{0,4},{4,8},{8,12},{12,16},{16,20},{20,24},{24,28},{1,5},{5,9},{9,... | collective-permute-start | bytes 1572872 | tf_op jit(solution)/shard_map/ppermute | solution.py:20
  95.9 1.3 copy-start.49
  96.2 1.3 copy-start.48
  96.5 1.3 copy-start.47
  96.9 1.3 copy-start.46
  97.2 1.3 copy-start.45
  97.5 1.3 copy-start.44
  97.8 1.3 copy-start.43
  98.1 1.3 copy-start.42
  98.5 1.3 copy-start.41
  98.8 1.3 copy-start.40
  99.1 1.3 copy-start.39
  99.4 1.3 copy-start.38
  99.7 1.3 copy-start.37
  100.0 1.3 copy-start.36
  100.4 1.3 copy-start.35
  100.7 1.3 copy-start.34
  101.0 1.3 copy-start.33
  101.3 1.3 copy-start.32
  101.6 1.3 copy-start.31
  101.9 1.3 copy-start.30
  102.3 1.3 copy-start.29
  102.6 1.3 copy-start.28
  102.9 1.2 copy-start.27
  136.1 3.7 %copy-start.1 = (bf16[27,64,256]{2,1,0:T(8,128)(2,1)S(1)}, bf16[27,64,256]{2,1,0:T(8,128)(2,1)}, u32[]{:S(2)}) copy-start(bf16[27,64,256]{2,1,0:T(8,128)(2,1)} %param.5) | copy-start | bytes 2654212
  (18 other events, 20.2 us)
Sparse Core Ops, SparseCore 0:
  106.0 96.0 all-reduce.3
where the time goes:
time: 212 us
  waiting for transfers between devices  65.1 us (31%)
  blocking collectives  44.4 us (21%)
  local copies, waits for them, and re-layouts  42.4 us (20%)
  matrix products  25 us (12%)
  starting transfers between devices  16.8 us (8%)
  between operations  14.9 us (7%)
  other arithmetic  3.07 us (1%)
    psum x1, waiting for transfers between devices, body(): filter_grad, bias_grad = lax.psum((filter_part, bias_part), 'space')  53.6 us
    psum x1, blocking collectives, body(): filter_grad, bias_grad = lax.psum((filter_part, bias_part), 'space')  28.3 us
    slice x6, local copies, waits for them, and re-layouts, window(): lax.slice(padded, (0, depth_off, row_off, col_off), (chans, depth_off + p...  19.5 us
    all_gather x2, blocking collectives, all_channels(): return lax.all_gather(volume, 'chan', axis=0, tiled=True)  16.1 us
    unnamed x126, local copies, waits for them, and re-layouts  13.7 us
    ppermute x2, waiting for transfers between devices, extended(): lax.ppermute(tail, axis, [(i, (i + 1) % count) for i in range(ends)])  11 us
    ppermute x2, starting transfers between devices, extended(): lax.ppermute(tail, axis, [(i, (i + 1) % count) for i in range(ends)])  10.7 us
    dot_general x27, matrix products, contract_lead(): lax.dot_general(left, right, (((0,), (0,)), ((), ())), preferred_element_...  9.24 us
  transfers between devices with their start and end apart: 6, of which 3 were waited for; matrix products, arithmetic and copies ran while one was open for 22% of the time, Pallas kernels for 0%

commit v1 on v0

--- a/solution.py
+++ b/solution.py
@@ -73,7 +73,10 @@
     voxels = planes * cells
     offsets = [(tap // 9, tap // 3 % 3, tap % 3) for tap in range(TAPS)]
     padded_all = plane_pad(full_view(features))
-    columns = lax.all_to_all(filters, "chan", split_axis=2, concat_axis=1, tiled=True)
+    columns = jnp.concatenate(
+        lax.all_to_all(jnp.stack(jnp.split(filters, lax.axis_size("chan"), axis=2)), "chan", 0, 0),
+        axis=1,
+    )
     summed = jnp.zeros((local_out, voxels), jnp.float32)
     for tap_index, (depth_off, row_off, col_off) in enumerate(offsets):
         piece = window(padded_all, depth_off, row_off, col_off, planes)

time: 212 us -> 205 us (0.967)
  local copies, waits for them, and re-layouts: 42.4 us -> 35.2 us
    squeeze x27 -> x0, local copies, waits for them, and re-layouts: 6.08 us -> none  [body(): summed = summed + contract_lead(columns[tap_index], piece)]
    psum x1, waiting for transfers between devices: 53.6 us -> 51.4 us  [body(): filter_grad, bias_grad = lax.psum((filter_part, bias_part), 'space')]
    unnamed x126 -> x115, local copies, waits for them, and re-layouts: 13.7 us -> 12.7 us
  transfers between devices with their start and end apart: 6 -> 6, of which waited for: 3 -> 3; matrix products, arithmetic and copies ran while one was open for 22% -> 23% of each run, Pallas kernels for 0% -> 0%
where the time goes in v1:
time: 205 us
  waiting for transfers between devices  64.6 us (32%)
  blocking collectives  44.5 us (22%)
  local copies, waits for them, and re-layouts  35.2 us (17%)
  matrix products  23.4 us (11%)
  starting transfers between devices  17.4 us (8%)
  between operations  14.9 us (7%)
  other arithmetic  4.86 us (2%)
    psum x1, waiting for transfers between devices, body(): filter_grad, bias_grad = lax.psum((filter_part, bias_part), 'space')  51.4 us
    psum x1, blocking collectives, body(): filter_grad, bias_grad = lax.psum((filter_part, bias_part), 'space')  28.4 us
    slice x6, local copies, waits for them, and re-layouts, window(): lax.slice(padded, (0, depth_off, row_off, col_off), (chans, depth_off + p...  19.1 us
    all_gather x2, blocking collectives, all_channels(): return lax.all_gather(volume, 'chan', axis=0, tiled=True)  16.1 us
    unnamed x115, local copies, waits for them, and re-layouts  12.7 us
    ppermute x2, waiting for transfers between devices, extended(): lax.ppermute(tail, axis, [(i, (i + 1) % count) for i in range(ends)])  11.1 us
    ppermute x2, starting transfers between devices, extended(): lax.ppermute(tail, axis, [(i, (i + 1) % count) for i in range(ends)])  10.6 us
    dot_general x27, matrix products, contract_last(): lax.dot_general(left, right, (((1,), (1,)), ((), ())), preferred_element_...  8.02 us
  transfers between devices with their start and end apart: 6, of which 3 were waited for; matrix products, arithmetic and copies ran while one was open for 23% of the time, Pallas kernels for 0%

profile of v1, /device:TPU:0, one launch (start us, length us, event | category | flops | bytes accessed | tf_op | source)
XLA Modules:
  0.0 204.8 jit_solution(13724851527920847361)
XLA Ops:
  7.2 9.0 %all_gather.6 = bf16[256,1,1024]{2,0,1:T(8,128)(2,1)S(1)} all-gather(bf16[64,1,1024]{2,0,1:T(8,128)(2,1)} %param.4), channel_id=1, replica_groups=mesh['space'=8,'chan'=4] {'chan'}, dimensions={0}, use_global_device_ids=true | all-gather | bytes 655360 | tf_op jit(solution)/shard_map/all_gather | solution.py:62
  16.2 1.0 copy.14
  17.2 1.3 collective-permute-start.1
  18.5 5.3 %collective-permute-start = (bf16[256,1,1024]{0,2,1:T(8,128)(2,1)}, bf16[256,1,1024]{0,2,1:T(8,128)(2,1)}, u32[]{:S(2)}, u32[]{:S(2)}) collective-permute-start(bf16[256,1,1024]{0,2,1:T(8,128)(2,1)} %copy.14), channel_id=1, source_target_pairs={{0,4},{4,8},{8,12},{12,16},{16,20},{20,24},{24,28},{1,5},{5,9},{9,... | collective-permute-start | bytes 1572872 | tf_op jit(solution)/shard_map/ppermute | solution.py:20
  23.8 0.4 slice_bitcast_fusion.3
  24.3 0.5 pad_maximum_fusion
  24.7 2.5 %reshape.422 = bf16[4,2,55296]{2,1,0:T(2,128)(2,1)} reshape(bf16[4,27,64,64]{3,2,1,0:T(8,128)(2,1)S(1)} %pad_maximum_fusion) | data formatting | bytes 1769472
  27.2 4.2 %all-to-all-start = ((bf16[4,2,55296]{2,1,0:T(2,128)(2,1)}), bf16[4,2,55296]{2,1,0:T(2,128)(2,1)}, u32[]{:S(2)}, u32[]{:S(2)}) async-start(bf16[4,2,55296]{2,1,0:T(2,128)(2,1)} %reshape.422), calls=%async_computation | async-start | bytes 1769472 | tf_op jit(solution)/shard_map/all_to_all | solution.py:77
  31.5 2.0 collective-permute-done.1
  33.6 11.1 %collective-permute-done = bf16[256,1,1024]{0,2,1:T(8,128)(2,1)} collective-permute-done((bf16[256,1,1024]{0,2,1:T(8,128)(2,1)}, bf16[256,1,1024]{0,2,1:T(8,128)(2,1)}, u32[]{:S(2)}, u32[]{:S(2)}) %collective-permute-start) | collective-permute-done | bytes 524320 | tf_op jit(solution)/shard_map/ppermute | solution.py:20
  44.7 1.5 pad_maximum_fusion.1
  46.2 3.4 %pad_dynamic-slice_fusion.15 = (bf16[64,1,32,32]{0,3,2,1:T(8,128)(2,1)}, bf16[64,1,32,32]{0,3,2,1:T(8,128)(2,1)}, bf16[64,1,32,32]{0,3,2,1:T(8,128)(2,1)}, bf16[...) fusion(s32[]{:T(128)S(6)} %select_n.3, ...), kind=kLoop, calls=%fused_computation.15 | loop fusion | bytes 3014668 | tf_op jit(solution)/shard_map/slice | solution.py:37
  49.6 4.5 %pad_dynamic-slice_fusion.26 = (bf16[64,1,32,32]{0,3,2,1:T(8,128)(2,1)S(1)}, bf16[64,1,32,32]{0,3,2,1:T(8,128)(2,1)}, bf16[64,1,32,32]{0,3,2,1:T(8,128)(2,1)}, b...) fusion(s32[]{:T(128)S(6)} %select_n.3, ...), kind=kLoop, calls=%fused_computation.26 | loop fusion | bytes 3670028 | tf_op jit(solution)/shard_map/slice | solution.py:37
  54.2 2.1 %pad_slice_fusion.1 = (bf16[256,1,32,32]{0,3,2,1:T(8,128)(2,1)S(1)}, bf16[256,1,32,32]{0,3,2,1:T(8,128)(2,1)}, bf16[256,1,32,32]{0,3,2,1:T(8,128)(2,1)}, bf16[25...) fusion(bf16[256,3,32,32]{0,3,2,1:T(8,128)(2,1)S(1)} %bitcast.500), kind=kLoop, calls=%fused_computation.28 | loop fusion | bytes 7340032 | tf_op jit(solution)/shard_map/slice | solution.py:37
  56.2 4.6 %pad_slice_fusion = (bf16[256,1,32,32]{0,3,2,1:T(8,128)(2,1)}, bf16[256,1,32,32]{0,3,2,1:T(8,128)(2,1)}, bf16[256,1,32,32]{0,3,2,1:T(8,128)(2,1)}, bf16[256,1,32...) fusion(bf16[256,3,32,32]{0,3,2,1:T(8,128)(2,1)S(1)} %bitcast.501), kind=kLoop, calls=%fused_computation.27 | loop fusion | bytes 11534336 | tf_op jit(solution)/shard_map/slice | solution.py:37
  60.9 2.9 %reshape.423 = bf16[4,27,64,64]{3,2,1,0:T(8,128)(2,1)S(1)} reshape(bf16[4,2,55296]{2,1,0:T(2,128)(2,1)} %all-to-all-done) | data formatting | bytes 1769472
  64.0 0.8 copy-done.25
  74.0 0.3 fusion.41
  74.3 7.1 %all-gather = bf16[256,1024]{1,0:T(8,128)(2,1)S(1)} all-gather(bf16[64,1024]{1,0:T(8,128)(2,1)S(1)} %get-tuple-element.128), channel_id=2, replica_groups=mesh['space'=8,'chan'=4] {'chan'}, dimensions={0}, use_global_device_ids=true | all-gather | bytes 655360 | tf_op jit(solution)/shard_map/all_gather | solution.py:62
  81.4 1.3 collective-permute-start.3
  82.7 5.2 %collective-permute-start.2 = (bf16[256,1,1024]{2,0,1:T(8,128)(2,1)S(1)}, bf16[256,1,1024]{2,0,1:T(8,128)(2,1)S(1)}, u32[]{:S(2)}, u32[]{:S(2)}) collective-permute-start(bf16[256,1,1024]{2,0,1:T(8,128)(2,1)S(1)} %bitcast.496), channel_id=1, source_target_pairs={{0,4},{4,8},{8,12},{12,16},{16,20},{20,24},{24,28},{1,5},{5,9},{9,... | collective-permute-start | bytes 1572872 | tf_op jit(solution)/shard_map/ppermute | solution.py:20
  87.9 1.0 copy.18
  89.6 0.3 fusion.37
  89.9 0.3 fusion.36
  90.2 0.3 fusion.35
  91.1 0.3 fusion.32
  91.5 0.3 fusion.31
  92.1 0.3 fusion.29
  92.4 0.3 fusion.28
  92.7 0.3 fusion.27
  93.4 0.3 fusion.25
  93.7 0.3 fusion.24
  94.3 0.3 fusion.22
  94.6 0.3 fusion.21
  95.0 0.3 fusion.20
  95.6 0.3 fusion.18
  96.2 0.3 fusion.16
  96.5 0.3 fusion.15
  96.8 0.3 fusion.14
  97.4 1.4 broadcast_multiply_fusion
  99.0 28.4 %psum.15 = f32[256]{0:T(256)} all-reduce(f32[256]{0:T(256)S(1)} %broadcast_multiply_fusion.1), channel_id=1, replica_groups=mesh['space'=8,'chan'=4] {'space'}, use_global_device_ids=true, to_apply=%region_2.3 | all-reduce | flops 256 | bytes 2048 | tf_op jit(solution)/shard_map/psum | solution.py:110
  127.4 1.3 pad_maximum_fusion.2
  128.7 1.7 copy.17
  130.4 0.9 pad_slice_fusion.25
  131.3 3.7 %pad_slice_fusion.24 = (bf16[256,1,32,32]{0,3,2,1:T(8,128)(2,1)S(1)}, bf16[256,1,32,32]{0,3,2,1:T(8,128)(2,1)S(1)}, bf16[256,1,32,32]{0,3,2,1:T(8,128)(2,1)S(1)}...) fusion(bf16[256,3,32,32]{0,3,2,1:T(8,128)(2,1)S(1)} %bitcast.503), kind=kLoop, calls=%fused_computation.51 | loop fusion | bytes 11534336 | tf_op jit(solution)/shard_map/slice | solution.py:37
  142.7 1.0 copy.19
  143.7 51.4 %all-reduce.4.cloned.1.call-done = f32[27,64,256]{2,1,0:T(8,128)} async-done(((f32[27,64,256]{2,1,0:T(8,128)}), f32[27,64,256]{2,1,0:T(8,128)}) %all-reduce.4.cloned.1.call-update) | async-done | bytes 1769488 | tf_op jit(solution)/shard_map/psum | solution.py:110
  195.1 2.9 %copy.47 = f32[27,64,256]{2,1,0:T(8,128)} copy(f32[27,64,256]{2,1,0:T(8,128)} %all-reduce.4.cloned.1.call-done) | data formatting | bytes 3538944
  (181 shorter events, 20.0 us)
Async XLA Ops:
  7.2 16.7 %copy-start = (bf16[27,64,256]{2,1,0:T(8,128)(2,1)S(1)}, bf16[27,64,256]{2,1,0:T(8,128)(2,1)}, u32[]{:S(2)}) copy-start(bf16[27,64,256]{2,1,0:T(8,128)(2,1)} %param.5) | copy-start | bytes 2654212
  17.2 16.4 %collective-permute-start.1 = (bf16[256,1,1024]{0,2,1:T(8,128)(2,1)}, bf16[256,1,1024]{0,2,1:T(8,128)(2,1)}, u32[]{:S(2)}, u32[]{:S(2)}) collective-permute-start(bf16[256,1,1024]{0,2,1:T(8,128)(2,1)} %copy.14), channel_id=1, source_target_pairs={{4,0},{8,4},{12,8},{16,12},{20,16},{24,20},{28,24},{5,1},{9,5},{13... | collective-permute-start | bytes 1572872 | tf_op jit(solution)/shard_map/ppermute | solution.py:22
  18.5 26.2 %collective-permute-start = (bf16[256,1,1024]{0,2,1:T(8,128)(2,1)}, bf16[256,1,1024]{0,2,1:T(8,128)(2,1)}, u32[]{:S(2)}, u32[]{:S(2)}) collective-permute-start(bf16[256,1,1024]{0,2,1:T(8,128)(2,1)} %copy.14), channel_id=1, source_target_pairs={{0,4},{4,8},{8,12},{12,16},{16,20},{20,24},{24,28},{1,5},{5,9},{9,... | collective-permute-start | bytes 1572872 | tf_op jit(solution)/shard_map/ppermute | solution.py:20
  27.2 33.6 %all-to-all-start = ((bf16[4,2,55296]{2,1,0:T(2,128)(2,1)}), bf16[4,2,55296]{2,1,0:T(2,128)(2,1)}, u32[]{:S(2)}, u32[]{:S(2)}) async-start(bf16[4,2,55296]{2,1,0:T(2,128)(2,1)} %reshape.422), calls=%async_computation | async-start | bytes 1769472 | tf_op jit(solution)/shard_map/all_to_all | solution.py:77
  31.5 163.6 %all-reduce.4.cloned.1.call-start = ((), (), s32[]{:S(2)}) async-start(), calls=%async_computation.1 | async-start | bytes 3538944 | tf_op jit(solution)/shard_map/psum | solution.py:110
  63.8 1.3 copy-start.7
  63.8 1.6 copy-start.24
  64.0 1.7 copy-start.23
  66.0 1.2 copy-start.20
  67.1 1.1 copy-start.17
  67.5 1.2 copy-start.16
  68.5 1.1 copy-start.14
  68.9 1.2 copy-start.13
  69.6 1.1 copy-start.11
  70.0 1.1 copy-start.10
  70.3 1.1 copy-start.9
  71.0 1.1 copy-start.4
  71.4 1.1 copy-start.3
  71.8 1.1 copy-start.2
  72.1 1.1 copy-start.1
  73.8 15.1 %copy-start.51 = (bf16[64,1,32,32]{0,3,2,1:T(8,128)(2,1)S(1)}, bf16[64,1,32,32]{0,3,2,1:T(8,128)(2,1)}, u32[]{:S(2)}) copy-start(bf16[64,1,32,32]{0,3,2,1:T(8,128)(2,1)} %get-tuple-element.69) | copy-start | bytes 393220
  73.9 15.3 %copy-start.50 = (bf16[64,1,32,32]{0,3,2,1:T(8,128)(2,1)S(1)}, bf16[64,1,32,32]{0,3,2,1:T(8,128)(2,1)}, u32[]{:S(2)}) copy-start(bf16[64,1,32,32]{0,3,2,1:T(8,128)(2,1)} %get-tuple-element.68) | copy-start | bytes 393220
  74.3 15.3 %copy-start.49 = (bf16[64,1,32,32]{0,3,2,1:T(8,128)(2,1)S(1)}, bf16[64,1,32,32]{0,3,2,1:T(8,128)(2,1)}, u32[]{:S(2)}) copy-start(bf16[64,1,32,32]{0,3,2,1:T(8,128)(2,1)} %get-tuple-element.67) | copy-start | bytes 393220
  74.3 15.6 %copy-start.48 = (bf16[64,1,32,32]{0,3,2,1:T(8,128)(2,1)S(1)}, bf16[64,1,32,32]{0,3,2,1:T(8,128)(2,1)}, u32[]{:S(2)}) copy-start(bf16[64,1,32,32]{0,3,2,1:T(8,128)(2,1)} %get-tuple-element.66) | copy-start | bytes 393220
  81.4 46.0 %collective-permute-start.3 = (bf16[256,1,1024]{2,0,1:T(8,128)(2,1)S(1)}, bf16[256,1,1024]{2,0,1:T(8,128)(2,1)S(1)}, u32[]{:S(2)}, u32[]{:S(2)}) collective-permute-start(bf16[256,1,1024]{2,0,1:T(8,128)(2,1)S(1)} %bitcast.495), channel_id=1, source_target_pairs={{4,0},{8,4},{12,8},{16,12},{20,16},{24,20},{28,24},{5,1},{9,5},{13... | collective-permute-start | bytes 1572872 | tf_op jit(solution)/shard_map/ppermute | solution.py:22
  82.7 44.7 %collective-permute-start.2 = (bf16[256,1,1024]{2,0,1:T(8,128)(2,1)S(1)}, bf16[256,1,1024]{2,0,1:T(8,128)(2,1)S(1)}, u32[]{:S(2)}, u32[]{:S(2)}) collective-permute-start(bf16[256,1,1024]{2,0,1:T(8,128)(2,1)S(1)} %bitcast.496), channel_id=1, source_target_pairs={{0,4},{4,8},{8,12},{12,16},{16,20},{20,24},{24,28},{1,5},{5,9},{9,... | collective-permute-start | bytes 1572872 | tf_op jit(solution)/shard_map/ppermute | solution.py:20
  88.9 1.3 copy-start.47
  89.2 1.3 copy-start.46
  89.5 1.3 copy-start.45
  89.9 1.3 copy-start.44
  90.2 1.3 copy-start.43
  90.5 1.3 copy-start.42
  90.8 1.3 copy-start.41
  91.1 1.3 copy-start.40
  91.4 1.3 copy-start.39
  91.8 1.3 copy-start.38
  92.1 1.3 copy-start.37
  92.4 1.3 copy-start.36
  92.7 1.3 copy-start.35
  93.0 1.3 copy-start.34
  93.4 1.3 copy-start.33
  93.7 1.3 copy-start.32
  94.0 1.3 copy-start.31
  94.3 1.3 copy-start.30
  94.6 1.3 copy-start.29
  94.9 1.3 copy-start.28
  95.3 1.3 copy-start.27
  95.6 1.2 copy-start.26
  (13 other events, 14.5 us)
Sparse Core Ops, SparseCore 0:
  98.9 96.1 all-reduce.3
